TPU v7x, 32 devices: a whole 2x2x4 slice. The times are simulated.
32 devices in a mesh: rows: 4 (over y, x), cols: 8 (over z, core).
Axes of the slice: x: 2, y: 2, z: 4, core: 2. Of those that a mesh axis runs over, the one named last changes fastest.
Arguments:
- weight: float32 [3072, 16384], P(('rows', 'cols')), may hold values from -6 to 6
- factor_panel: float32 [4, 8, 512, 1024], P(None, 'cols'), may hold values from -0.1875 to 0.1875
- diag_inverse: float32 [2, 512, 512], P(None, 'rows'), may hold values from -2 to 2, as said below
Outputs:
- whitened: float32 [3072, 4, 8, 512], P('rows', None, 'cols')
Inputs may be any that keep to these rules, and one draw needn't show every extreme that they name: `diag_inverse`: each of the two blocks is lower triangular with diagonal entries between 0.5 and 2.
All inputs are finite; a program needn't handle non-finite values.
Results may differ from a plain program's by a relative error of at most 0.00007.
Values sent between devices are 32-bit elements; how exact they have to be, the bound alone decides.
A program may use at most 64 MiB of HBM per device.

v0:
```python
import functools

import jax
import jax.numpy as jnp
from jax import lax
from jax.experimental import pallas as pl
from jax.experimental.pallas import tpu as pltpu
from jax.sharding import PartitionSpec as P

LANES = 128
TILE = 256
SEND_SEMS = 200
WRITES = 8
VMEM_LIMIT = 50 * 10**6


def split(x):
    high = x.astype(jnp.bfloat16)
    low = (x - high.astype(jnp.float32)).astype(jnp.bfloat16)
    return high, low


def times_transpose(left_high, left_low, right):
    right_high, right_low = split(right)
    dot = functools.partial(
        lax.dot_general,
        dimension_numbers=(((1,), (1,)), ((), ())),
        preferred_element_type=jnp.float32,
    )
    return dot(left_high, right_high) + (dot(left_high, right_low) + dot(left_low, right_high))


def arrived(ref, sem):
    pltpu.make_async_copy(ref, ref, sem).wait()


def kernel(
    n_rows, n_cols, weight, panel, inverse_part, stage,
    lead, land, panel_full, inverse, bridge, a_high, a_low, x_high, x_low, solved, product,
    send_sem, lead_sem, bridge_first_sem, bridge_sem, inverse_sem, land_sem, panel_sem, present_sem,
):
    row, me = lax.axis_index("rows"), lax.axis_index("cols")
    chips = n_cols // 2
    z, core = me // 2, me % 2
    sibling = me + 1 - 2 * core
    part = weight.shape[0]
    cycles, block = panel.shape[0], panel.shape[2]
    share = block // n_rows
    width = cycles * block // LANES

    barrier = pltpu.get_barrier_semaphore()
    has_lower, has_upper = z > 0, z < chips - 1

    def greet(sem, device):
        pl.semaphore_signal(sem, inc=1, device_id=device, device_id_type=pl.DeviceIdType.MESH)

    for other in range(2):
        pl.when(has_upper)(lambda other=other: greet(barrier, (row, 2 * (z + 1) + other)))
        pl.when(has_lower)(lambda other=other: greet(barrier, (row, 2 * (z - 1) + other)))
    greet(barrier, (row, sibling))
    for step in range(1, n_rows):
        greet(barrier, ((row + step) % n_rows, me))

    def part_rows(source):
        return pl.ds(pl.multiple_of(source * part, part), part)

    def column_block(h, c):
        return pl.ds(pl.multiple_of((h * n_cols + c) * block, block), block)

    my_share = pl.ds(pl.multiple_of(row * share, share), share)

    pl.semaphore_wait(barrier, n_rows + jnp.where(has_upper, 2, 0) + jnp.where(has_lower, 2, 0))

    sent = []

    def send(condition, source, target, recv_sem, device):
        slot = send_sem.at[len(sent)]

        def copy():
            return pltpu.make_async_remote_copy(
                src_ref=source,
                dst_ref=target,
                send_sem=slot,
                recv_sem=recv_sem,
                device_id=device,
                device_id_type=pl.DeviceIdType.MESH,
            )

        sent.append((condition, copy))
        if condition is None:
            copy().start()
        else:
            pl.when(condition)(lambda: copy().start())

    def send_lead(condition, source_id, target_col, from_weight=False):
        source = weight.at[:, pl.ds(0, 2 * block)] if from_weight else lead.at[part_rows(source_id), :]
        send(condition, source, lead.at[part_rows(source_id), :], lead_sem.at[source_id], (row, target_col))

    def send_bridge(condition, target_col, from_panel=False):
        source = panel.at[0, 0, my_share, pl.ds(0, block)] if from_panel else bridge.at[my_share, :]
        send(condition, source, bridge.at[my_share, :], bridge_first_sem.at[0], (row, target_col))

    def send_blocks(condition, target_col):
        for h in range(cycles):
            needed = condition
            if h == 0:
                needed = target_col > 1 if condition is None else condition & (target_col > 1)
            send(
                needed,
                weight.at[:, column_block(h, target_col)],
                land.at[h, part_rows(me), :],
                land_sem.at[me, h],
                (row, target_col),
            )

    send_bridge(me == 1, me + 2, True)
    send_lead(z < chips - 1, me, me + 2, True)
    send_lead(z > 0, me, me - 2, True)
    send_bridge(me == 1, sibling, True)
    send_lead(None, me, sibling, True)
    def forward(distance):
        left, right = me - 2 * distance, me + 2 * distance
        has_left, has_right = z >= distance, z + distance < chips

        pl.when(has_left)(lambda: arrived(lead.at[part_rows(left), :], lead_sem.at[left]))
        send_lead(has_left & (z < chips - 1), left, me + 2)
        send_lead(has_left, left, sibling)
        carries = left == 1
        pl.when(carries)(lambda: arrived(bridge.at[my_share, :], bridge_first_sem.at[0]))
        send_bridge(carries & (z < chips - 1), me + 2)
        send_bridge(carries, sibling)
        pl.when(has_right)(lambda: arrived(lead.at[part_rows(right), :], lead_sem.at[right]))
        send_lead(has_right & (z > 0), right, me - 2)
        send_lead(has_right, right, sibling)

    def rest_of_inputs():
        for step in range(1, n_rows):
            send(
                None,
                inverse_part,
                inverse.at[:, my_share, :],
                inverse_sem.at[row],
                ((row + step) % n_rows, me),
            )
        pltpu.make_async_copy(weight.at[:, pl.ds(0, 2 * block)], lead.at[part_rows(me), :], lead_sem.at[me]).start()
        pltpu.make_async_copy(inverse_part, inverse.at[:, my_share, :], inverse_sem.at[row]).start()

        def own_first():
            return pltpu.make_async_copy(
                panel.at[0, 0, my_share, pl.ds(0, block)], bridge.at[my_share, :], bridge_first_sem.at[0]
            )

        pl.when(me == 1)(lambda: own_first().start())
        for h in range(cycles):
            own = pltpu.make_async_copy(
                weight.at[:, column_block(h, me)], land.at[h, part_rows(me), :], land_sem.at[me, h]
            )
            if h == 0:
                pl.when(me > 1)(own.start)
            else:
                own.start()
            pltpu.make_async_copy(panel.at[h, 0], panel_full.at[h], panel_sem.at[h]).start()

    def tell(distance):
        if distance < chips - 1:
            pl.when((z >= distance) & has_upper)(lambda: greet(present_sem.at[0, distance + 1], (row, me + 2)))
            pl.when((z + distance < chips) & has_lower)(
                lambda: greet(present_sem.at[1, distance + 1], (row, me - 2))
            )

    def meet_far():
        tell(1)
        for distance in range(2, chips):
            pl.when(z >= distance)(lambda: pl.semaphore_wait(present_sem.at[0, distance], 1))
            pl.when(z + distance < chips)(lambda: pl.semaphore_wait(present_sem.at[1, distance], 1))
            tell(distance)

    turn = 0
    for distance in range(1, chips):
        for other in range(2):
            if turn == 1:
                send_blocks(None, sibling)
            if turn == 2:
                meet_far()
            for side in (1, -1):
                chip = z + side * distance
                exists = chip < chips if side == 1 else chip >= 0
                send_blocks(exists, 2 * chip + (core + other) % 2)
            if turn == 0:
                rest_of_inputs()
            turn += 1
            if turn < chips:
                forward(turn)

    pl.when((core == 0) | (me == 1))(lambda: arrived(bridge.at[my_share, :], bridge_first_sem.at[0]))
    for step in range(1, n_rows):
        send(
            None,
            bridge.at[my_share, :],
            bridge.at[my_share, :],
            bridge_sem.at[row],
            ((row + step) % n_rows, me),
        )

    arrived(lead.at[part_rows(me), :], lead_sem.at[me])
    for chip in range(chips):
        source = 2 * chip + 1 - core
        arrived(lead.at[part_rows(source), :], lead_sem.at[source])
    for source in range(n_rows):
        rows = pl.ds(source * share, share)
        arrived(inverse.at[:, rows, :], inverse_sem.at[source])

    @pl.loop(0, n_cols)
    def _(source):
        rows = part_rows(source)
        a_high[rows, :], a_low[rows, :] = split(lead[rows, :block])

    def tile(index, base=0):
        return pl.ds(pl.multiple_of(base + index * TILE, TILE), TILE)

    def solve(which):
        @pl.loop(0, block // TILE)
        def _(index):
            value = times_transpose(a_high[...], a_low[...], inverse[which, tile(index), :])
            columns = tile(index, which * block)
            solved[:, columns] = value
            x_high[:, columns], x_low[:, columns] = split(value)

    solve(0)
    for step in range(1, n_rows):
        source = (row + step) % n_rows
        rows = pl.ds(pl.multiple_of(source * share, share), share)
        arrived(bridge.at[rows, :], bridge_sem.at[source])

    @pl.loop(0, block // TILE)
    def _(index):
        value = lead[:, tile(index, block)] - times_transpose(
            x_high[:, :block], x_low[:, :block], bridge[tile(index), :]
        )
        a_high[:, tile(index)], a_low[:, tile(index)] = split(value)

    solve(1)
    for h in range(cycles):
        arrived(panel_full.at[h], panel_sem.at[h])

    @pl.loop(0, cycles)
    def _(h):
        @pl.loop(0, block // TILE)
        def _(index):
            product[h, :, tile(index)] = times_transpose(x_high[...], x_low[...], panel_full[h, tile(index), :])

    reach = jnp.minimum(z, chips - 1 - z)
    far_side = jnp.where(z < chips - 1 - z, 1, -1)

    @pl.loop(0, n_cols)
    def _(position):
        place = position // 2
        near = (place + 1) // 2 * (2 * (place % 2) - 1)
        far = (place - reach) * far_side
        chip = z + jnp.where(place <= 2 * reach, near, far)
        source = 2 * chip + (core + position) % 2
        rows = part_rows(source)

        def store(h, value):
            for q in range(block // LANES):
                first = source * (part * width) + (h * (block // LANES) + q)
                stage[pl.ds(first, part, stride=width), :] = value[:, q * LANES : (q + 1) * LANES]

        def update(h):
            arrived(land.at[h, rows, :], land_sem.at[source, h])
            store(h, land[h, rows, :] - product[h, rows, :])

        for h in range(cycles):
            if h == 0:
                pl.when(me == 0)(lambda: store(0, solved[rows, :block]))
                pl.when(me == 1)(lambda: store(0, solved[rows, block:]))
                pl.when(me > 1)(lambda: update(0))
            else:
                update(h)

    for condition, copy in sent:
        if condition is None:
            copy().wait_send()
        else:
            pl.when(condition)(lambda copy=copy: copy().wait_send())


def write_out(staged, out, sem):
    rows = staged.shape[0] // WRITES
    copies = [
        pltpu.make_async_copy(staged.at[pl.ds(i * rows, rows), :], out.at[pl.ds(i * rows, rows), :], sem.at[i])
        for i in range(WRITES)
    ]
    for copy in copies:
        copy.start()
    for copy in copies:
        copy.wait()


def solution(mesh):
    n_rows, n_cols = mesh.shape["rows"], mesh.shape["cols"]

    def per_device(weight, factor_panel, diag_inverse):
        part = weight.shape[0]
        cycles, _, block, depth = factor_panel.shape
        group = n_cols * part
        width = cycles * block // LANES
        vmem = pltpu.VMEM
        f32, bf16 = jnp.float32, jnp.bfloat16
        result = pl.pallas_call(
            functools.partial(kernel, n_rows, n_cols),
            out_shape=pltpu.VMEM((group * width, LANES), f32),
            in_specs=[pl.BlockSpec(memory_space=pltpu.HBM)] * 3,
            out_specs=pl.BlockSpec(memory_space=pltpu.VMEM),
            scratch_shapes=[
                vmem((group, 2 * block), f32),
                vmem((cycles, group, block), f32),
                vmem((cycles, block, depth), f32),
                vmem((2, block, block), f32),
                vmem((block, block), f32),
                vmem((group, block), bf16),
                vmem((group, block), bf16),
                vmem((group, depth), bf16),
                vmem((group, depth), bf16),
                vmem((group, depth), f32),
                vmem((cycles, group, block), f32),
                pltpu.SemaphoreType.DMA((SEND_SEMS,)),
                pltpu.SemaphoreType.DMA((n_cols,)),
                pltpu.SemaphoreType.DMA((1,)),
                pltpu.SemaphoreType.DMA((n_rows,)),
                pltpu.SemaphoreType.DMA((n_rows,)),
                pltpu.SemaphoreType.DMA((n_cols, cycles)),
                pltpu.SemaphoreType.DMA((cycles,)),
                pltpu.SemaphoreType.REGULAR((2, n_cols // 2)),
            ],
            compiler_params=pltpu.CompilerParams(
                collective_id=0, has_side_effects=True, vmem_limit_bytes=VMEM_LIMIT
            ),
        )(weight, factor_panel, diag_inverse)
        result = pl.pallas_call(
            write_out,
            out_shape=jax.ShapeDtypeStruct(result.shape, f32),
            in_specs=[pl.BlockSpec(memory_space=pltpu.VMEM)],
            out_specs=pl.BlockSpec(memory_space=pltpu.HBM),
            scratch_shapes=[pltpu.SemaphoreType.DMA((WRITES,))],
            compiler_params=pltpu.CompilerParams(vmem_limit_bytes=2**20),
        )(result)
        return result.reshape(group, cycles, 1, block)

    placed = (P(("rows", "cols"), None), P(None, "cols", None, None), P(None, "rows", None))
    return jax.shard_map(
        per_device,
        mesh=mesh,
        in_specs=placed,
        out_specs=P("rows", None, "cols", None),
        check_vma=False,
    )
```

profile of v0, /device:TPU:25, one launch (start us, length us, event | category | flops | bytes accessed | tf_op | source)
XLA Modules:
  0.0 162.8 jit_solution(7173198182342369378)
XLA Ops:
  0.0 160.0 %shard_map.37.staged = f32[12288,128]{1,0:T(8,128)S(1)} custom-call(f32[96,16384]{1,0:T(8,128)} %weight.1, f32[4,1,512,1024]{3,2,1,0:T(8,128)} %panel.1, f32[2,128,512]{2,1,0:T(8,128)} %inverse_part.1), custom_call_target="tpu_custom_call" | custom-call | tf_op jit(solution)/shard_map/pallas_call | solution.py:310
  160.0 2.7 %shard_map.38 = f32[12288,128]{1,0:T(8,128)} custom-call(f32[12288,128]{1,0:T(8,128)S(1)} %shard_map.37.staged), custom_call_target="tpu_custom_call" | custom-call | tf_op jit(solution)/shard_map/pallas_call | solution.py:340
where the time goes:
time: 164 us; the launch traced here: 163 us
  Pallas kernels  163 us (99%)
    pallas_call x1, Pallas kernels, per_device(): pl.pallas_call(functools.partial(kernel, n_rows, n_cols), out_shape=pltpu...  160 us

commit v1 on v0

--- a/solution.py
+++ b/solution.py
@@ -9,7 +9,8 @@
 
 LANES = 128
 TILE = 256
-SEND_SEMS = 200
+SEND_CLASSES = 6
+BLOCKS, LEADS, SIBLING_LEADS, HALVES, INVERSES, SHARES = range(SEND_CLASSES)
 WRITES = 8
 VMEM_LIMIT = 50 * 10**6
 
@@ -37,7 +38,7 @@
 def kernel(
     n_rows, n_cols, weight, panel, inverse_part, stage,
     lead, land, panel_full, inverse, bridge, a_high, a_low, x_high, x_low, solved, product,
-    send_sem, lead_sem, bridge_first_sem, bridge_sem, inverse_sem, land_sem, panel_sem, present_sem,
+    send_sem, lead_sem, half_sem, bridge_sem, inverse_sem, land_sem, panel_sem, present_sem, rows_sem,
 ):
     row, me = lax.axis_index("rows"), lax.axis_index("cols")
     chips = n_cols // 2
@@ -46,6 +47,8 @@
     part = weight.shape[0]
     cycles, block = panel.shape[0], panel.shape[2]
     share = block // n_rows
+    half = share // 2
+    others = n_rows - 1
     width = cycles * block // LANES
 
     barrier = pltpu.get_barrier_semaphore()
@@ -58,8 +61,12 @@
         pl.when(has_upper)(lambda other=other: greet(barrier, (row, 2 * (z + 1) + other)))
         pl.when(has_lower)(lambda other=other: greet(barrier, (row, 2 * (z - 1) + other)))
     greet(barrier, (row, sibling))
-    for step in range(1, n_rows):
-        greet(barrier, ((row + step) % n_rows, me))
+    def greet_rows(sem):
+        for step in range(1, n_rows):
+            greet(sem, ((row + step) % n_rows, me))
+
+    even = z % 2 == 0
+    pl.when(even)(lambda: greet_rows(barrier))
 
     def part_rows(source):
         return pl.ds(pl.multiple_of(source * part, part), part)
@@ -69,36 +76,38 @@
 
     my_share = pl.ds(pl.multiple_of(row * share, share), share)
 
-    pl.semaphore_wait(barrier, n_rows + jnp.where(has_upper, 2, 0) + jnp.where(has_lower, 2, 0))
-
-    sent = []
-
-    def send(condition, source, target, recv_sem, device):
-        slot = send_sem.at[len(sent)]
-
-        def copy():
-            return pltpu.make_async_remote_copy(
+    pl.semaphore_wait(
+        barrier, 1 + jnp.where(even, others, 0) + jnp.where(has_upper, 2, 0) + jnp.where(has_lower, 2, 0)
+    )
+
+    def send(condition, source, target, kind, recv_sem, device):
+        def start():
+            pltpu.make_async_remote_copy(
                 src_ref=source,
                 dst_ref=target,
-                send_sem=slot,
+                send_sem=send_sem.at[kind],
                 recv_sem=recv_sem,
                 device_id=device,
                 device_id_type=pl.DeviceIdType.MESH,
-            )
-
-        sent.append((condition, copy))
+            ).start()
+
         if condition is None:
-            copy().start()
+            start()
         else:
-            pl.when(condition)(lambda: copy().start())
+            pl.when(condition)(start)
 
     def send_lead(condition, source_id, target_col, from_weight=False):
         source = weight.at[:, pl.ds(0, 2 * block)] if from_weight else lead.at[part_rows(source_id), :]
-        send(condition, source, lead.at[part_rows(source_id), :], lead_sem.at[source_id], (row, target_col))
-
-    def send_bridge(condition, target_col, from_panel=False):
-        source = panel.at[0, 0, my_share, pl.ds(0, block)] if from_panel else bridge.at[my_share, :]
-        send(condition, source, bridge.at[my_share, :], bridge_first_sem.at[0], (row, target_col))
+        kind = SIBLING_LEADS if target_col is sibling else LEADS
+        send(condition, source, lead.at[part_rows(source_id), :], kind, lead_sem.at[source_id], (row, target_col))
+
+    def half_rows(which):
+        return pl.ds(pl.multiple_of(row * share + which * half, half), half)
+
+    def send_half(condition, which, target_col, from_panel=False):
+        rows = half_rows(which)
+        source = panel.at[0, 0, rows, pl.ds(0, block)] if from_panel else bridge.at[rows, :]
+        send(condition, source, bridge.at[rows, :], HALVES, half_sem.at[which], (row, target_col))
 
     def send_blocks(condition, target_col):
         for h in range(cycles):
@@ -109,15 +118,18 @@
                 needed,
                 weight.at[:, column_block(h, target_col)],
                 land.at[h, part_rows(me), :],
-                land_sem.at[me, h],
+                BLOCKS,
+                land_sem.at[me, h // (cycles - 1)],
                 (row, target_col),
             )
 
-    send_bridge(me == 1, me + 2, True)
     send_lead(z < chips - 1, me, me + 2, True)
     send_lead(z > 0, me, me - 2, True)
-    send_bridge(me == 1, sibling, True)
+    send_half(me == 1, 0, sibling, True)
+    send_half(me == 1, 1, me + 2, True)
+    send_half(me == 1, 1, sibling, True)
     send_lead(None, me, sibling, True)
+
     def forward(distance):
         left, right = me - 2 * distance, me + 2 * distance
         has_left, has_right = z >= distance, z + distance < chips
@@ -125,41 +137,50 @@
         pl.when(has_left)(lambda: arrived(lead.at[part_rows(left), :], lead_sem.at[left]))
         send_lead(has_left & (z < chips - 1), left, me + 2)
         send_lead(has_left, left, sibling)
-        carries = left == 1
-        pl.when(carries)(lambda: arrived(bridge.at[my_share, :], bridge_first_sem.at[0]))
-        send_bridge(carries & (z < chips - 1), me + 2)
-        send_bridge(carries, sibling)
+        carries = z == distance
+        pl.when(carries)(lambda: arrived(bridge.at[half_rows(core), :], half_sem.at[core]))
+        send_half(carries & (z < chips - 1), core, me + 2)
+        send_half(carries, core, sibling)
         pl.when(has_right)(lambda: arrived(lead.at[part_rows(right), :], lead_sem.at[right]))
         send_lead(has_right & (z > 0), right, me - 2)
         send_lead(has_right, right, sibling)
 
     def rest_of_inputs():
+        pltpu.make_async_copy(weight.at[:, pl.ds(0, 2 * block)], lead.at[part_rows(me), :], lead_sem.at[me]).start()
+        pltpu.make_async_copy(inverse_part, inverse.at[:, my_share, :], inverse_sem.at[0]).start()
+
+        for which in range(2):
+            own_half = pltpu.make_async_copy(
+                panel.at[0, 0, half_rows(which), pl.ds(0, block)], bridge.at[half_rows(which), :], half_sem.at[which]
+            )
+            pl.when(me == 1)(own_half.start)
+        for h in range(cycles):
+            own = pltpu.make_async_copy(
+                weight.at[:, column_block(h, me)], land.at[h, part_rows(me), :], land_sem.at[me, h // (cycles - 1)]
+            )
+            if h == 0:
+                pl.when(me > 1)(own.start)
+            else:
+                own.start()
+            pltpu.make_async_copy(panel.at[h, 0], panel_full.at[h], panel_sem.at[0]).start()
+        pl.when(me == 0)(lambda: arrived(bridge.at[half_rows(0), :], half_sem.at[0]))
+        send_half(me == 0, 0, me + 2)
+
+    def meet_rows():
+        below = even & has_upper
+        pl.when(below)(lambda: greet_rows(rows_sem.at[0]))
+        pl.when(below)(lambda: pl.semaphore_wait(rows_sem.at[0], others))
+        pl.when(below)(lambda: greet(rows_sem.at[1], (row, me + 2)))
+        pl.when(z % 2 == 1)(lambda: pl.semaphore_wait(rows_sem.at[1], 1))
         for step in range(1, n_rows):
             send(
                 None,
                 inverse_part,
                 inverse.at[:, my_share, :],
-                inverse_sem.at[row],
+                INVERSES,
+                inverse_sem.at[0],
                 ((row + step) % n_rows, me),
             )
-        pltpu.make_async_copy(weight.at[:, pl.ds(0, 2 * block)], lead.at[part_rows(me), :], lead_sem.at[me]).start()
-        pltpu.make_async_copy(inverse_part, inverse.at[:, my_share, :], inverse_sem.at[row]).start()
-
-        def own_first():
-            return pltpu.make_async_copy(
-                panel.at[0, 0, my_share, pl.ds(0, block)], bridge.at[my_share, :], bridge_first_sem.at[0]
-            )
-
-        pl.when(me == 1)(lambda: own_first().start())
-        for h in range(cycles):
-            own = pltpu.make_async_copy(
-                weight.at[:, column_block(h, me)], land.at[h, part_rows(me), :], land_sem.at[me, h]
-            )
-            if h == 0:
-                pl.when(me > 1)(own.start)
-            else:
-                own.start()
-            pltpu.make_async_copy(panel.at[h, 0], panel_full.at[h], panel_sem.at[h]).start()
 
     def tell(distance):
         if distance < chips - 1:
@@ -188,17 +209,21 @@
                 send_blocks(exists, 2 * chip + (core + other) % 2)
             if turn == 0:
                 rest_of_inputs()
+                meet_rows()
             turn += 1
             if turn < chips:
                 forward(turn)
 
-    pl.when((core == 0) | (me == 1))(lambda: arrived(bridge.at[my_share, :], bridge_first_sem.at[0]))
+    pl.when((z > 0) | (me == 0))(lambda: arrived(bridge.at[half_rows(1 - core), :], half_sem.at[1 - core]))
+    for which in range(2):
+        pl.when(me == 1)(lambda which=which: arrived(bridge.at[half_rows(which), :], half_sem.at[which]))
     for step in range(1, n_rows):
         send(
             None,
             bridge.at[my_share, :],
             bridge.at[my_share, :],
-            bridge_sem.at[row],
+            SHARES,
+            bridge_sem.at[0],
             ((row + step) % n_rows, me),
         )
 
@@ -206,9 +231,7 @@
     for chip in range(chips):
         source = 2 * chip + 1 - core
         arrived(lead.at[part_rows(source), :], lead_sem.at[source])
-    for source in range(n_rows):
-        rows = pl.ds(source * share, share)
-        arrived(inverse.at[:, rows, :], inverse_sem.at[source])
+    arrived(inverse, inverse_sem.at[0])
 
     @pl.loop(0, n_cols)
     def _(source):
@@ -227,10 +250,7 @@
             x_high[:, columns], x_low[:, columns] = split(value)
 
     solve(0)
-    for step in range(1, n_rows):
-        source = (row + step) % n_rows
-        rows = pl.ds(pl.multiple_of(source * share, share), share)
-        arrived(bridge.at[rows, :], bridge_sem.at[source])
+    arrived(bridge.at[pl.ds(0, others * share), :], bridge_sem.at[0])
 
     @pl.loop(0, block // TILE)
     def _(index):
@@ -240,8 +260,7 @@
         a_high[:, tile(index)], a_low[:, tile(index)] = split(value)
 
     solve(1)
-    for h in range(cycles):
-        arrived(panel_full.at[h], panel_sem.at[h])
+    arrived(panel_full, panel_sem.at[0])
 
     @pl.loop(0, cycles)
     def _(h):
@@ -266,23 +285,45 @@
                 first = source * (part * width) + (h * (block // LANES) + q)
                 stage[pl.ds(first, part, stride=width), :] = value[:, q * LANES : (q + 1) * LANES]
 
+        def landed(first, count):
+            part_of = land.at[pl.ds(first, count), rows, :]
+            arrived(part_of, land_sem.at[source, first // (cycles - 1)])
+
         def update(h):
-            arrived(land.at[h, rows, :], land_sem.at[source, h])
             store(h, land[h, rows, :] - product[h, rows, :])
 
-        for h in range(cycles):
-            if h == 0:
-                pl.when(me == 0)(lambda: store(0, solved[rows, :block]))
-                pl.when(me == 1)(lambda: store(0, solved[rows, block:]))
-                pl.when(me > 1)(lambda: update(0))
-            else:
-                update(h)
-
-    for condition, copy in sent:
-        if condition is None:
-            copy().wait_send()
-        else:
-            pl.when(condition)(lambda copy=copy: copy().wait_send())
+        pl.when(me > 1)(lambda: landed(0, cycles - 1))
+        if cycles > 2:
+            pl.when(me <= 1)(lambda: landed(1, cycles - 2))
+        pl.when(me == 0)(lambda: store(0, solved[rows, :block]))
+        pl.when(me == 1)(lambda: store(0, solved[rows, block:]))
+        pl.when(me > 1)(lambda: update(0))
+        for h in range(1, cycles):
+            if h == cycles - 1:
+                landed(h, 1)
+            update(h)
+
+    def left(kind, condition, view):
+        pl.when(condition)(lambda: arrived(view, send_sem.at[kind]))
+
+    def blocks_wide(count):
+        return weight.at[:, pl.ds(0, count * block)]
+
+    def bridge_rows(count):
+        return bridge.at[pl.ds(0, count), :]
+
+    count = (n_cols - 1) * cycles
+    left(BLOCKS, me > 1, blocks_wide(count - 2))
+    left(BLOCKS, me <= 1, blocks_wide(count - 1))
+    inner = has_lower & has_upper
+    left(LEADS, inner, blocks_wide(2 * (chips + 1)))
+    left(LEADS, jnp.logical_not(inner), blocks_wide(2))
+    arrived(blocks_wide(2 * chips), send_sem.at[SIBLING_LEADS])
+    left(HALVES, me == 1, bridge_rows(3 * half))
+    left(HALVES, (me == 0) | (z == chips - 1), bridge_rows(half))
+    left(HALVES, inner, bridge_rows(2 * half))
+    arrived(inverse.at[:, pl.ds(0, others * share), :], send_sem.at[INVERSES])
+    arrived(bridge_rows(others * share), send_sem.at[SHARES])
 
 
 def write_out(staged, out, sem):
@@ -324,14 +365,15 @@
                 vmem((group, depth), bf16),
                 vmem((group, depth), f32),
                 vmem((cycles, group, block), f32),
-                pltpu.SemaphoreType.DMA((SEND_SEMS,)),
+                pltpu.SemaphoreType.DMA((SEND_CLASSES,)),
                 pltpu.SemaphoreType.DMA((n_cols,)),
+                pltpu.SemaphoreType.DMA((2,)),
                 pltpu.SemaphoreType.DMA((1,)),
-                pltpu.SemaphoreType.DMA((n_rows,)),
-                pltpu.SemaphoreType.DMA((n_rows,)),
-                pltpu.SemaphoreType.DMA((n_cols, cycles)),
-                pltpu.SemaphoreType.DMA((cycles,)),
+                pltpu.SemaphoreType.DMA((1,)),
+                pltpu.SemaphoreType.DMA((n_cols, 2)),
+                pltpu.SemaphoreType.DMA((1,)),
                 pltpu.SemaphoreType.REGULAR((2, n_cols // 2)),
+                pltpu.SemaphoreType.REGULAR((2,)),
             ],
             compiler_params=pltpu.CompilerParams(
                 collective_id=0, has_side_effects=True, vmem_limit_bytes=VMEM_LIMIT

time: 164 us -> 162 us (0.988)
  no operation moved by 1% of the time
where the time goes in v1:
time: 162 us
  Pallas kernels  162 us (100%)
    pallas_call x1, Pallas kernels, per_device(): pl.pallas_call(functools.partial(kernel, n_rows, n_cols), out_shape=pltpu...  159 us

profile of v1, /device:TPU:25, one launch (start us, length us, event | category | flops | bytes accessed | tf_op | source)
XLA Modules:
  0.0 161.7 jit_solution(10270684035766301967)
XLA Ops:
  0.0 159.0 %shard_map.37.staged = f32[12288,128]{1,0:T(8,128)S(1)} custom-call(f32[96,16384]{1,0:T(8,128)} %weight.1, f32[4,1,512,1024]{3,2,1,0:T(8,128)} %panel.1, f32[2,128,512]{2,1,0:T(8,128)} %inverse_part.1), custom_call_target="tpu_custom_call" | custom-call | tf_op jit(solution)/shard_map/pallas_call | solution.py:351
  159.0 2.7 %shard_map.38 = f32[12288,128]{1,0:T(8,128)} custom-call(f32[12288,128]{1,0:T(8,128)S(1)} %shard_map.37.staged), custom_call_target="tpu_custom_call" | custom-call | tf_op jit(solution)/shard_map/pallas_call | solution.py:382

commit v2 on v1

--- a/solution.py
+++ b/solution.py
@@ -7,11 +7,10 @@
 from jax.experimental.pallas import tpu as pltpu
 from jax.sharding import PartitionSpec as P
 
-LANES = 128
 TILE = 256
 SEND_CLASSES = 6
 BLOCKS, LEADS, SIBLING_LEADS, HALVES, INVERSES, SHARES = range(SEND_CLASSES)
-WRITES = 8
+WRITES = 2
 VMEM_LIMIT = 50 * 10**6
 
 
@@ -49,7 +48,6 @@
     share = block // n_rows
     half = share // 2
     others = n_rows - 1
-    width = cycles * block // LANES
 
     barrier = pltpu.get_barrier_semaphore()
     has_lower, has_upper = z > 0, z < chips - 1
@@ -119,7 +117,7 @@
                 weight.at[:, column_block(h, target_col)],
                 land.at[h, part_rows(me), :],
                 BLOCKS,
-                land_sem.at[me, h // (cycles - 1)],
+                land_sem.at[me],
                 (row, target_col),
             )
 
@@ -156,7 +154,7 @@
             pl.when(me == 1)(own_half.start)
         for h in range(cycles):
             own = pltpu.make_async_copy(
-                weight.at[:, column_block(h, me)], land.at[h, part_rows(me), :], land_sem.at[me, h // (cycles - 1)]
+                weight.at[:, column_block(h, me)], land.at[h, part_rows(me), :], land_sem.at[me]
             )
             if h == 0:
                 pl.when(me > 1)(own.start)
@@ -184,16 +182,16 @@
 
     def tell(distance):
         if distance < chips - 1:
-            pl.when((z >= distance) & has_upper)(lambda: greet(present_sem.at[0, distance + 1], (row, me + 2)))
+            pl.when((z >= distance) & has_upper)(lambda: greet(present_sem.at[0, distance - 1], (row, me + 2)))
             pl.when((z + distance < chips) & has_lower)(
-                lambda: greet(present_sem.at[1, distance + 1], (row, me - 2))
+                lambda: greet(present_sem.at[1, distance - 1], (row, me - 2))
             )
 
     def meet_far():
         tell(1)
         for distance in range(2, chips):
-            pl.when(z >= distance)(lambda: pl.semaphore_wait(present_sem.at[0, distance], 1))
-            pl.when(z + distance < chips)(lambda: pl.semaphore_wait(present_sem.at[1, distance], 1))
+            pl.when(z >= distance)(lambda: pl.semaphore_wait(present_sem.at[0, distance - 2], 1))
+            pl.when(z + distance < chips)(lambda: pl.semaphore_wait(present_sem.at[1, distance - 2], 1))
             tell(distance)
 
     turn = 0
@@ -280,27 +278,21 @@
         source = 2 * chip + (core + position) % 2
         rows = part_rows(source)
 
+        def landed(first):
+            arrived(land.at[pl.ds(first, cycles - first), rows, :], land_sem.at[source])
+
         def store(h, value):
-            for q in range(block // LANES):
-                first = source * (part * width) + (h * (block // LANES) + q)
-                stage[pl.ds(first, part, stride=width), :] = value[:, q * LANES : (q + 1) * LANES]
-
-        def landed(first, count):
-            part_of = land.at[pl.ds(first, count), rows, :]
-            arrived(part_of, land_sem.at[source, first // (cycles - 1)])
+            stage[h, rows, :] = value
 
         def update(h):
             store(h, land[h, rows, :] - product[h, rows, :])
 
-        pl.when(me > 1)(lambda: landed(0, cycles - 1))
-        if cycles > 2:
-            pl.when(me <= 1)(lambda: landed(1, cycles - 2))
+        pl.when(me > 1)(lambda: landed(0))
+        pl.when(me <= 1)(lambda: landed(1))
         pl.when(me == 0)(lambda: store(0, solved[rows, :block]))
         pl.when(me == 1)(lambda: store(0, solved[rows, block:]))
         pl.when(me > 1)(lambda: update(0))
         for h in range(1, cycles):
-            if h == cycles - 1:
-                landed(h, 1)
             update(h)
 
     def left(kind, condition, view):
@@ -327,15 +319,13 @@
 
 
 def write_out(staged, out, sem):
-    rows = staged.shape[0] // WRITES
-    copies = [
-        pltpu.make_async_copy(staged.at[pl.ds(i * rows, rows), :], out.at[pl.ds(i * rows, rows), :], sem.at[i])
-        for i in range(WRITES)
-    ]
-    for copy in copies:
-        copy.start()
-    for copy in copies:
-        copy.wait()
+    cycles, group, _ = staged.shape
+    rows = group // WRITES
+    for h in range(cycles):
+        for i in range(WRITES):
+            some = pl.ds(i * rows, rows)
+            pltpu.make_async_copy(staged.at[h, some, :], out.at[some, h, 0, :], sem.at[0]).start()
+    pltpu.make_async_copy(staged, staged, sem.at[0]).wait()
 
 
 def solution(mesh):
@@ -345,12 +335,11 @@
         part = weight.shape[0]
         cycles, _, block, depth = factor_panel.shape
         group = n_cols * part
-        width = cycles * block // LANES
         vmem = pltpu.VMEM
         f32, bf16 = jnp.float32, jnp.bfloat16
         result = pl.pallas_call(
             functools.partial(kernel, n_rows, n_cols),
-            out_shape=pltpu.VMEM((group * width, LANES), f32),
+            out_shape=pltpu.VMEM((cycles, group, block), f32),
             in_specs=[pl.BlockSpec(memory_space=pltpu.HBM)] * 3,
             out_specs=pl.BlockSpec(memory_space=pltpu.VMEM),
             scratch_shapes=[
@@ -370,24 +359,23 @@
                 pltpu.SemaphoreType.DMA((2,)),
                 pltpu.SemaphoreType.DMA((1,)),
                 pltpu.SemaphoreType.DMA((1,)),
-                pltpu.SemaphoreType.DMA((n_cols, 2)),
+                pltpu.SemaphoreType.DMA((n_cols,)),
                 pltpu.SemaphoreType.DMA((1,)),
-                pltpu.SemaphoreType.REGULAR((2, n_cols // 2)),
+                pltpu.SemaphoreType.REGULAR((2, n_cols // 2 - 2)),
                 pltpu.SemaphoreType.REGULAR((2,)),
             ],
             compiler_params=pltpu.CompilerParams(
                 collective_id=0, has_side_effects=True, vmem_limit_bytes=VMEM_LIMIT
             ),
         )(weight, factor_panel, diag_inverse)
-        result = pl.pallas_call(
+        return pl.pallas_call(
             write_out,
-            out_shape=jax.ShapeDtypeStruct(result.shape, f32),
+            out_shape=jax.ShapeDtypeStruct((group, cycles, 1, block), f32),
             in_specs=[pl.BlockSpec(memory_space=pltpu.VMEM)],
             out_specs=pl.BlockSpec(memory_space=pltpu.HBM),
-            scratch_shapes=[pltpu.SemaphoreType.DMA((WRITES,))],
+            scratch_shapes=[pltpu.SemaphoreType.DMA((1,))],
             compiler_params=pltpu.CompilerParams(vmem_limit_bytes=2**20),
         )(result)
-        return result.reshape(group, cycles, 1, block)
 
     placed = (P(("rows", "cols"), None), P(None, "cols", None, None), P(None, "rows", None))
     return jax.shard_map(

time: 162 us -> 161 us (level)
  no operation moved by 1% of the time
where the time goes in v2:
time: 161 us
  Pallas kernels  161 us (100%)
    pallas_call x1, Pallas kernels, per_device(): pl.pallas_call(functools.partial(kernel, n_rows, n_cols), out_shape=pltpu...  158 us

profile of v2, /device:TPU:25, one launch (start us, length us, event | category | flops | bytes accessed | tf_op | source)
XLA Modules:
  0.0 160.9 jit_solution(17702660339700650708)
XLA Ops:
  0.0 158.2 %shard_map.37.staged = f32[4,768,512]{2,1,0:T(8,128)S(1)} custom-call(f32[96,16384]{1,0:T(8,128)} %weight.1, f32[4,1,512,1024]{3,2,1,0:T(8,128)} %panel.1, f32[2,128,512]{2,1,0:T(8,128)} %inverse_part.1), custom_call_target="tpu_custom_call" | custom-call | tf_op jit(solution)/shard_map/pallas_call | solution.py:340
  158.2 2.7 %shard_map.38 = f32[768,4,1,512]{3,2,1,0:T(1,128)} custom-call(f32[4,768,512]{2,1,0:T(8,128)S(1)} %shard_map.37.staged), custom_call_target="tpu_custom_call" | custom-call | tf_op jit(solution)/shard_map/pallas_call | solution.py:371

commit v3 on v2

--- a/solution.py
+++ b/solution.py
@@ -46,7 +46,8 @@
     part = weight.shape[0]
     cycles, block = panel.shape[0], panel.shape[2]
     share = block // n_rows
-    half = share // 2
+    split_at = share * 3 // 64 * 8
+    halves = split_at, share - split_at
     others = n_rows - 1
 
     barrier = pltpu.get_barrier_semaphore()
@@ -100,7 +101,7 @@
         send(condition, source, lead.at[part_rows(source_id), :], kind, lead_sem.at[source_id], (row, target_col))
 
     def half_rows(which):
-        return pl.ds(pl.multiple_of(row * share + which * half, half), half)
+        return pl.ds(pl.multiple_of(row * share + which * split_at, 8), halves[which])
 
     def send_half(condition, which, target_col, from_panel=False):
         rows = half_rows(which)
@@ -136,9 +137,11 @@
         send_lead(has_left & (z < chips - 1), left, me + 2)
         send_lead(has_left, left, sibling)
         carries = z == distance
-        pl.when(carries)(lambda: arrived(bridge.at[half_rows(core), :], half_sem.at[core]))
-        send_half(carries & (z < chips - 1), core, me + 2)
-        send_half(carries, core, sibling)
+        for which in range(2):
+            on_chain = carries & (core == which)
+            pl.when(on_chain)(lambda which=which: arrived(bridge.at[half_rows(which), :], half_sem.at[which]))
+            send_half(on_chain & (z < chips - 1), which, me + 2)
+            send_half(on_chain, which, sibling)
         pl.when(has_right)(lambda: arrived(lead.at[part_rows(right), :], lead_sem.at[right]))
         send_lead(has_right & (z > 0), right, me - 2)
         send_lead(has_right, right, sibling)
@@ -212,9 +215,9 @@
             if turn < chips:
                 forward(turn)
 
-    pl.when((z > 0) | (me == 0))(lambda: arrived(bridge.at[half_rows(1 - core), :], half_sem.at[1 - core]))
     for which in range(2):
-        pl.when(me == 1)(lambda which=which: arrived(bridge.at[half_rows(which), :], half_sem.at[which]))
+        pending = (me == 1) | (((z > 0) | (me == 0)) & (core != which))
+        pl.when(pending)(lambda which=which: arrived(bridge.at[half_rows(which), :], half_sem.at[which]))
     for step in range(1, n_rows):
         send(
             None,
@@ -311,9 +314,11 @@
     left(LEADS, inner, blocks_wide(2 * (chips + 1)))
     left(LEADS, jnp.logical_not(inner), blocks_wide(2))
     arrived(blocks_wide(2 * chips), send_sem.at[SIBLING_LEADS])
-    left(HALVES, me == 1, bridge_rows(3 * half))
-    left(HALVES, (me == 0) | (z == chips - 1), bridge_rows(half))
-    left(HALVES, inner, bridge_rows(2 * half))
+    left(HALVES, me == 1, bridge_rows(halves[0] + 2 * halves[1]))
+    left(HALVES, me == 0, bridge_rows(halves[0]))
+    for which in range(2):
+        left(HALVES, (core == which) & (z == chips - 1), bridge_rows(halves[which]))
+        left(HALVES, (core == which) & inner, bridge_rows(2 * halves[which]))
     arrived(inverse.at[:, pl.ds(0, others * share), :], send_sem.at[INVERSES])
     arrived(bridge_rows(others * share), send_sem.at[SHARES])
 

time: 161 us -> 161 us (level)
  no operation moved by 1% of the time
where the time goes in v3:
time: 161 us
  Pallas kernels  161 us (100%)
    pallas_call x1, Pallas kernels, per_device(): pl.pallas_call(functools.partial(kernel, n_rows, n_cols), out_shape=pltpu...  158 us

profile of v3, /device:TPU:25, one launch (start us, length us, event | category | flops | bytes accessed | tf_op | source)
XLA Modules:
  0.0 161.1 jit_solution(12441740328953567490)
XLA Ops:
  0.0 158.4 %shard_map.37.staged = f32[4,768,512]{2,1,0:T(8,128)S(1)} custom-call(f32[96,16384]{1,0:T(8,128)} %weight.1, f32[4,1,512,1024]{3,2,1,0:T(8,128)} %panel.1, f32[2,128,512]{2,1,0:T(8,128)} %inverse_part.1), custom_call_target="tpu_custom_call" | custom-call | tf_op jit(solution)/shard_map/pallas_call | solution.py:345
  158.4 2.7 %shard_map.38 = f32[768,4,1,512]{3,2,1,0:T(1,128)} custom-call(f32[4,768,512]{2,1,0:T(8,128)S(1)} %shard_map.37.staged), custom_call_target="tpu_custom_call" | custom-call | tf_op jit(solution)/shard_map/pallas_call | solution.py:376
